TPU v7x, 128 devices: a whole 4x4x4 slice. The times are simulated.
128 devices in a mesh: row: 8 (over x_hi, y), col: 16 (over x_lo, z, core).
Axes of the slice: x: 4 (x_hi: 2, x_lo: 2; x = x_hi * 2 + x_lo), y: 4, z: 4, core: 2. Of those that a mesh axis runs over, the one named last changes fastest.
Arguments:
- latent: bfloat16 [256, 81920], P('row', 'col'), may hold values from -6 to 6
- tile_reach: int32 [8, 16, 4], replicated, may hold values from 1 to 4
- first_weight: bfloat16 [3, 3, 320, 320], replicated, may hold values from -0.109375 to 0.109375
- first_bias: float32 [320], replicated, may hold values from -3 to 3
- second_weight: bfloat16 [3, 3, 320, 320], replicated, may hold values from -0.109375 to 0.109375
- second_bias: float32 [320], replicated, may hold values from -3 to 3
- proj_weight: bfloat16 [320, 512], replicated, may hold values from -0.3125 to 0.3125
- upper_weight: bfloat16 [3, 3, 512, 512], replicated, may hold values from -0.09375 to 0.09375
- upper_bias: float32 [512], replicated, may hold values from -3 to 3
- lower_weight: bfloat16 [3, 3, 512, 512], replicated, may hold values from -0.09375 to 0.09375
- lower_bias: float32 [512], replicated, may hold values from -3 to 3
Outputs:
- decoded: bfloat16 [512, 512, 512], P(('row', 'col'))
All inputs are finite; a program needn't handle non-finite values.
Results may differ from a plain program's by a relative error of at most 0.0065.
Values may be sent and summed in bfloat16 or wider, within the bound.
A program may use at most 64 MiB of HBM per device.

v0:
```python
import functools

import jax
import jax.numpy as jnp
from jax import lax
from jax.experimental import pallas as pl
from jax.experimental.pallas import tpu as pltpu
from jax.sharding import PartitionSpec as P

MARGIN = 4
SIDE = 8
PAD = 8
F32 = jnp.float32
BF = jnp.bfloat16
MESH = pl.DeviceIdType.MESH
VM = pl.BlockSpec(memory_space=pltpu.VMEM)
HB = pl.BlockSpec(memory_space=pltpu.HBM)
SM = pl.BlockSpec(memory_space=pltpu.SMEM)
AROUND = [(dr, dc) for dr in (-1, 0, 1) for dc in (-1, 0, 1) if (dr, dc) != (0, 0)]


def dot(a, b):
    return jnp.dot(a, b, preferred_element_type=F32)


def peer(row, col, dr, dc):
    rows, cols = lax.axis_size("row"), lax.axis_size("col")
    return lax.rem(row + (dr + rows), rows), lax.rem(col + (dc + cols), cols)


def place(reach_ref, row, col, dr, dc, rows, cols):
    n_row, n_col = lax.axis_size("row"), lax.axis_size("col")
    there = (row + dr >= 0) & (row + dr < n_row) & (col + dc >= 0) & (col + dc < n_col)
    r = lax.rem(row + (dr + n_row), n_row)
    c = lax.rem(col + (dc + n_col), n_col)
    low_r = jnp.maximum((row + dr) * rows - reach_ref[r, 0, c], 0)
    high_r = jnp.minimum((row + dr + 1) * rows + reach_ref[r, 1, c], rows * n_row)
    low_c = jnp.maximum((col + dc) * cols - reach_ref[r, 2, c], 0)
    high_c = jnp.minimum((col + dc + 1) * cols + reach_ref[r, 3, c], cols * n_col)
    return low_r, jnp.where(there, high_r, low_r), low_c, high_c


def spread(g):
    outer = 0.5 * (g[0] + g[2])
    mid = 0.5 * g[1]
    return [g[0], outer + mid, outer - mid, g[2]]


def upper_forms(up, out, sl, ln):
    cols = []
    for b in range(3):
        w = [up[a, b, sl, ln].astype(F32) for a in range(3)]
        cols.append([w[0], w[0] + w[1] + w[2], w[2]])
    for p in range(3):
        v = [cols[0][p], cols[0][p] + cols[1][p] + cols[2][p], cols[2][p]]
        for q in range(3):
            out[3 * p + q, sl, ln] = v[q].astype(BF)


def lower_forms(lo, out, sl, ln):
    cols = [spread([lo[a, b, sl, ln].astype(F32) for a in range(3)]) for b in range(3)]
    for r in range(4):
        v = spread([cols[b][r] for b in range(3)])
        for c in range(4):
            out[4 * r + c, sl, ln] = v[c].astype(BF)


def front_kernel(
    reach_ref, lat_ref, w1_hbm, b1_ref, w2_hbm, b2_ref, up_hbm, lo_hbm, out_ref, oux_ref, uo_hbm, vo_hbm, *refs
):
    lands, strips = refs[:8], refs[8:16]
    core_ref, side, side2, stage, x, act, ga, rest, w1, w2, r1, r2, y_ref, can, canx, count_ref, up, lo, uo, vo = refs[16:36]
    send0, recv0, send, recv, send2, recv2, sendx, recvx, self_sem, wsem, usem, vsem = refs[36:]
    rows, cols, ch = core_ref.shape
    m = MARGIN
    high, wide, span = rows + 2 * m, cols + 2 * SIDE, cols + 2 * m
    base = SIDE - m
    main = ch // 128 * 128
    left = ch - main
    part = 8
    row, col = lax.axis_index("row"), lax.axis_index("col")
    n_col = lax.axis_size("col")
    barrier = pltpu.get_barrier_semaphore()
    greet = [peer(row, col, 0, o) for o in range(1, n_col)]
    greet += [peer(row, col, dr, dc) for dr, dc in AROUND if dr != 0]
    for g in greet:
        pl.semaphore_signal(barrier, inc=1, device_id=g, device_id_type=MESH)
    loads = [
        pltpu.make_async_copy(src, dst, wsem.at[n])
        for n, (src, dst) in enumerate(((w1_hbm, w1), (w2_hbm, w2), (up_hbm, up), (lo_hbm, lo)))
    ]
    for c in loads[:2]:
        c.start()
    low_r, high_r, low_c, high_c = place(reach_ref, row, col, 0, 0, rows, cols)
    top, start = row * rows - m, col * cols - SIDE

    def put(dr, dc, at, num, value):
        lo_c, hi_c = {-1: (0, SIDE), 0: (SIDE, SIDE + cols), 1: (SIDE + cols, wide)}[dc]
        rid = lax.broadcasted_iota(jnp.int32, value.shape, 0) + (top + at)
        cid = lax.broadcasted_iota(jnp.int32, value.shape, 1) + (start + lo_c)
        ok = (rid >= low_r) & (rid < high_r) & (cid >= low_c) & (cid < high_c)
        x[pl.ds(at + 1, num), lo_c:hi_c] = jnp.where(ok, value.astype(F32), 0.0)

    def put_core(n, _):
        put(0, 0, m + part * n, part, core_ref[pl.ds(part * n, part)])
        return 0

    for c in range(cols):
        v = lat_ref[:, ch * c : ch * (c + 1)].astype(F32)
        for n in range(pl.cdiv(ch, 128)):
            size = min(128, ch - 128 * n)
            piece = v[:, 128 * n : 128 * n + size]
            if size < 128:
                piece = jnp.concatenate([piece, jnp.zeros((rows, 128 - size), F32)], axis=1)
            stage[n, pl.ds(c, rows, stride=cols), :] = piece
    for n in range(pl.cdiv(ch, 128)):
        size = min(128, ch - 128 * n)
        core_ref[:, :, 128 * n : 128 * n + size] = stage[n].reshape(rows, cols, 128)[:, :, :size].astype(BF)

    def turned(v):
        return jnp.concatenate([v[:, 4:8], v[:, 0:4]], axis=1)

    mid_row = rows // 2
    for n, at in ((0, cols - SIDE), (1, 0)):
        v = core_ref[:, at : at + SIDE].astype(F32)
        lo_half, hi_half = (turned(v[:mid_row]), v[mid_row:]) if n == 0 else (v[:mid_row], turned(v[mid_row:]))
        low_lanes = lax.broadcasted_iota(jnp.int32, lo_half.shape, 1) < m
        side[n] = jnp.where(low_lanes, lo_half, hi_half).astype(BF)
    pl.semaphore_wait(barrier, len(greet))
    halos = []
    for n, (dr, dc) in enumerate(AROUND):
        rs = {-1: pl.ds(rows - m, m), 0: pl.ds(0, rows), 1: pl.ds(0, m)}[dr]
        cs = {-1: pl.ds(cols - SIDE, SIDE), 0: pl.ds(0, cols), 1: pl.ds(0, SIDE)}[dc]
        halos.append(
            pltpu.make_async_remote_copy(
                src_ref=core_ref.at[rs, cs] if dr != 0 else side.at[0 if dc < 0 else 1],
                dst_ref=lands[n],
                send_sem=send0.at[n],
                recv_sem=recv0.at[n],
                device_id=peer(row, col, -dr, -dc),
                device_id_type=MESH,
            )
        )
        halos[-1].start()
    for c in loads[2:]:
        c.start()
    lax.fori_loop(0, rows // part, put_core, 0)
    for buf in (x, act):
        buf[0] = jnp.zeros((wide, ch), F32)
        buf[high + 1] = jnp.zeros((wide, ch), F32)

    def clear(n, _):
        act[pl.ds(part * n + 1, part), 0:8, :] = jnp.zeros((part, 8, ch), F32)
        act[pl.ds(part * n + 1, part), wide - 8 : wide, :] = jnp.zeros((part, 8, ch), F32)
        return 0

    lax.fori_loop(0, high // part, clear, 0)
    shape = count_ref.shape
    rid = lax.broadcasted_iota(jnp.int32, shape, 0) + (row * rows - 1)
    cid = lax.broadcasted_iota(jnp.int32, shape, 1) + col * cols
    total = jnp.zeros(shape, F32)
    for dr in (-1, 0, 1):
        for dc in (-1, 0, 1):
            lr, hr, lc, hc = place(reach_ref, row, col, dr, dc, rows, cols)
            inside = (rid >= lr) & (rid < hr) & (cid >= lc) & (cid < hc)
            total += jnp.where(inside, 1.0, 0.0)
    count_ref[...] = total

    def narrow(w, r):
        r[...] = jnp.concatenate([w[dr, :, main:] for dr in range(3)], axis=1)

    for c in loads[:2]:
        c.wait()
    narrow(w1, r1)
    narrow(w2, r2)
    for c in halos:
        c.wait()
    got = dict(zip(AROUND, lands))
    for dr, dc in AROUND:
        if dr == 0:

            def put_side(n, _):
                v = got[0, dc][pl.ds(part * n, part)].astype(F32)
                pair = (turned(v), v) if dc < 0 else (v, turned(v))
                put(0, dc, m + part * n, part, pair[0])
                put(0, dc, m + mid_row + part * n, part, pair[1])
                return 0

            lax.fori_loop(0, mid_row // part, put_side, 0)
        else:
            put(dr, dc, 0 if dr < 0 else m + rows, m, got[dr, dc][...])

    def gather(buf):
        def group(n, _):
            for k in range(3):
                at = 6 * n + 2 * k
                pieces = [
                    buf[pl.ds(at, 2), base + dc : base + dc + span, :].reshape(2 * span, ch) for dc in (-1, 0, 1)
                ]
                v = jnp.concatenate(pieces, axis=1).astype(BF)
                ga[pl.ds(pl.multiple_of(span * at, 16), 2 * span), :] = v
            return 0

        lax.fori_loop(0, (high + 2) // 6, group, 0)

    half = high // 2
    count = half * span

    def conv(w, r, b_ref, finish):
        for n in range(2):
            size = (high + 2) // 2 * span
            rest[pl.ds(n * size, size), :] = dot(ga[pl.ds(n * size, size), :], r[...])

        for n in range(2):
            at = n * count
            big = (
                dot(ga[pl.ds(at, count), :], w[0, :, :main])
                + dot(ga[pl.ds(at + span, count), :], w[1, :, :main])
                + dot(ga[pl.ds(at + 2 * span, count), :], w[2, :, :main])
            )
            finish(n, 0, main, big + b_ref[:main][None])
            small = (
                rest[pl.ds(at, count), :left]
                + rest[pl.ds(at + span, count), left : 2 * left]
                + rest[pl.ds(at + 2 * span, count), 2 * left :]
            )
            finish(n, main, ch, small + b_ref[main:][None])

    def window_mask(n, width):
        rid = lax.broadcasted_iota(jnp.int32, (half, 1, width), 0) + (top + n * half)
        kid = lax.broadcasted_iota(jnp.int32, (1, span, width), 1) + (start + base)
        row_one = jnp.where((rid >= low_r) & (rid < high_r), 1.0, 0.0)
        col_one = jnp.where((kid >= low_c) & (kid < high_c), 1.0, 0.0)
        return row_one * col_one

    def first(n, lo, hi, v):
        v = 0.5 * v
        v = (v + v * jnp.tanh(v)).reshape(half, span, hi - lo)
        act[pl.ds(n * half + 1, half), base : base + span, lo:hi] = v * window_mask(n, hi - lo)

    def second(n, lo, hi, v):
        here = pl.ds(n * half + 1, half)
        v = v.reshape(half, span, hi - lo) + x[here, base : base + span, lo:hi]
        act[here, base : base + span, lo:hi] = v * window_mask(n, hi - lo)

    gather(x)
    conv(w1, r1, b1_ref, first)
    gather(act)
    conv(w2, r2, b2_ref, second)

    def emit(n, _):
        y_ref[pl.ds(part * n, part)] = act[pl.ds(part * n + 1, part)].astype(BF)
        return 0

    lax.fori_loop(0, high // part, emit, 0)
    edge = m + 1
    tall = rows + 2
    cut = tall // 2
    for n, at in ((0, SIDE + cols), (1, 0)):
        v = act[pl.ds(m, cut), at : at + SIDE] + turned(act[pl.ds(m + cut, cut), at : at + SIDE])
        side2[n] = v.astype(BF)
    copies = []
    for n, (dr, dc) in enumerate(AROUND):
        rs = {-1: pl.ds(high - edge, edge), 0: pl.ds(m - 1, tall), 1: pl.ds(0, edge)}[dr]
        cs = {-1: pl.ds(SIDE + cols, SIDE), 0: pl.ds(SIDE, cols), 1: pl.ds(0, SIDE)}[dc]
        copies.append(
            pltpu.make_async_remote_copy(
                src_ref=y_ref.at[rs, cs] if dr != 0 else side2.at[0 if dc < 0 else 1],
                dst_ref=strips[n],
                send_sem=send.at[n],
                recv_sem=recv.at[n],
                device_id=peer(row, col, -dr, -dc),
                device_id_type=MESH,
            )
        )
        copies[-1].start()
    depth, width = up.shape[2:]
    block = 64
    stores = []

    def forms(form, src, dst, dst_hbm, sem):
        def store(n):
            sl = pl.ds(pl.multiple_of(n * block, block), block)
            return pltpu.make_async_copy(dst.at[:, sl], dst_hbm.at[:, sl], sem.at[n])

        def body(n, _):
            def inner(k, _):
                sl = pl.ds(pl.multiple_of(n * block + k * 16, 16), 16)
                for lane in range(0, width, 128):
                    form(src, dst, sl, slice(lane, lane + 128))
                return 0

            lax.fori_loop(0, block // 16, inner, 0)
            store(n).start()
            return 0

        lax.fori_loop(0, depth // block, body, 0)
        stores.extend(store(n) for n in range(depth // block))

    loads[2].wait()
    forms(upper_forms, up, uo, uo_hbm, usem)
    for c in copies:
        c.wait()
    got2 = dict(zip(AROUND, strips))

    main = 256

    def merge(lo_r, num, dr):
        here = pl.ds(lo_r, num)
        total = y_ref[pl.ds(m - 1 + lo_r, num), SIDE : SIDE + cols].astype(F32)
        late = lo_r >= cut
        there = pl.ds(lo_r - cut if late else lo_r, num)
        lhs, rhs = got2[0, -1][there].astype(F32), got2[0, 1][there].astype(F32)
        if late:
            lhs, rhs = turned(lhs), turned(rhs)
        low = lax.broadcasted_iota(jnp.int32, lhs.shape, 1) < m
        lhs, rhs = jnp.where(low, lhs, 0.0), jnp.where(low, 0.0, rhs)
        if dr:
            total += got2[dr, 0][...].astype(F32)
            lhs += got2[dr, -1][...].astype(F32)
            rhs += got2[dr, 1][...].astype(F32)
        total += jnp.concatenate([lhs, rhs], axis=1)
        n = count_ref[here][:, :, :1]
        total = jnp.where(n > 0, total / jnp.maximum(n, 1.0), 0.0)
        can[here] = total[:, :, :main].astype(BF)
        canx[here] = jnp.concatenate([total[:, :8, main:], total[:, 8:, main:]], axis=2).astype(BF)

    merge(0, edge, -1)
    merge(edge, cut - edge, 0)
    merge(cut, cut - edge, 0)
    merge(tall - edge, edge, 1)
    mine = pl.ds(pl.multiple_of(cols * col, cols), cols)
    step = rows // n_col
    deep = step + 2
    minex = pl.ds(pl.multiple_of(8 * col, 8), 8)
    own = [
        pltpu.make_async_copy(can.at[pl.ds(step * col, deep)], out_ref.at[:, mine], self_sem.at[0]),
        pltpu.make_async_copy(canx.at[pl.ds(step * col, deep)], oux_ref.at[:, minex], self_sem.at[1]),
    ]
    for c in own:
        c.start()

    def send_rows(to, at, spot, spotx, o):
        return [
            pltpu.make_async_remote_copy(
                src_ref=src.at[pl.ds(at, deep)],
                dst_ref=dst.at[:, where],
                send_sem=ss.at[o],
                recv_sem=rs.at[o],
                device_id=to,
                device_id_type=MESH,
            )
            for src, dst, where, ss, rs in (
                (can, out_ref, spot, send2, recv2),
                (canx, oux_ref, spotx, sendx, recvx),
            )
        ]

    copies = []
    for o in range(1, n_col):
        to = peer(row, col, 0, o)
        copies.append(send_rows(to, step * to[1], mine, minex, o))
        for c in copies[-1]:
            c.start()
    loads[3].wait()
    forms(lower_forms, lo, vo, vo_hbm, vsem)
    for c in stores:
        c.wait()
    for c in own:
        c.wait()
    for o in range(1, n_col):
        src = peer(row, col, 0, -o)
        spot = pl.ds(pl.multiple_of(cols * src[1], cols), cols)
        spotx = pl.ds(pl.multiple_of(8 * src[1], 8), 8)
        for c in copies[o - 1]:
            c.wait_send()
        for c in send_rows(src, 0, spot, spotx, o):
            c.wait_recv()


def front(reach, latent, w1, b1, w2, b2, upper, lower):
    ch = w1.shape[2]
    rows, cols = latent.shape[0], latent.shape[1] // ch
    d = upper.shape[2]
    m = MARGIN
    high, wide, span = rows + 2 * m, cols + 2 * SIDE, cols + 2 * m
    n_col = lax.axis_size("col")
    tall = rows + 2
    deep = rows // n_col + 2
    left = 3 * (ch % 128)
    w1, w2 = (w.reshape(3, 3 * ch, ch) for w in (w1, w2))

    def around(full, thin):
        return [pltpu.VMEM((full // 2 if dr == 0 else thin, cols if dc == 0 else SIDE, ch), BF) for dr, dc in AROUND]

    return pl.pallas_call(
        front_kernel,
        out_shape=[
            jax.ShapeDtypeStruct((deep, n_col * cols, 256), BF),
            jax.ShapeDtypeStruct((deep, n_col * 8, 128), BF),
            jax.ShapeDtypeStruct((9, d, d), BF),
            jax.ShapeDtypeStruct((16, d, d), BF),
        ],
        in_specs=[SM, VM, HB, VM, HB, VM, HB, HB],
        out_specs=[VM, VM, HB, HB],
        scratch_shapes=around(rows, m)
        + around(tall, m + 1)
        + [
            pltpu.VMEM((rows, cols, ch), BF),
            pltpu.VMEM((2, rows // 2, SIDE, ch), BF),
            pltpu.VMEM((2, tall // 2, SIDE, ch), BF),
            pltpu.VMEM((pl.cdiv(ch, 128), rows * cols, 128), F32),
            pltpu.VMEM((high + 2, wide, ch), F32),
            pltpu.VMEM((high + 2, wide, ch), F32),
            pltpu.VMEM(((high + 2) * span, 3 * ch), BF),
            pltpu.VMEM(((high + 2) * span, left), F32),
            pltpu.VMEM((3, 3 * ch, ch), BF),
            pltpu.VMEM((3, 3 * ch, ch), BF),
            pltpu.VMEM((3 * ch, left), BF),
            pltpu.VMEM((3 * ch, left), BF),
            pltpu.VMEM((high, wide, ch), BF),
            pltpu.VMEM((tall, cols, 256), BF),
            pltpu.VMEM((tall, 8, 128), BF),
            pltpu.VMEM((tall, cols, 128), F32),
            pltpu.VMEM((3, 3, d, d), BF),
            pltpu.VMEM((3, 3, d, d), BF),
            pltpu.VMEM((9, d, d), BF),
            pltpu.VMEM((16, d, d), BF),
        ]
        + [pltpu.SemaphoreType.DMA((8,))] * 4
        + [
            pltpu.SemaphoreType.DMA((n_col,)),
            pltpu.SemaphoreType.DMA((n_col,)),
            pltpu.SemaphoreType.DMA((n_col,)),
            pltpu.SemaphoreType.DMA((n_col,)),
            pltpu.SemaphoreType.DMA((2,)),
            pltpu.SemaphoreType.DMA((4,)),
            pltpu.SemaphoreType.DMA((d // 64,)),
            pltpu.SemaphoreType.DMA((d // 64,)),
        ],
        compiler_params=pltpu.CompilerParams(
            collective_id=0, has_side_effects=True, vmem_limit_bytes=60 * 2**20
        ),
        name="front",
    )(reach, latent, w1, b1, w2, b2, upper, lower)


def decode_kernel(cols, d, can_ref, canx_ref, proj_ref, uup_hbm, bup_ref, ulo_hbm, blo_ref, out_ref,
                  hid, act, ts, acc, inter, projx, obuf, uup, ulo, upsem, losem, osem):
    row, col = lax.axis_index("row"), lax.axis_index("col")
    first_dev = (row == 0) & (col == 0)
    last_dev = (row == lax.axis_size("row") - 1) & (col == lax.axis_size("col") - 1)
    upc = [pltpu.make_async_copy(uup_hbm.at[i], uup.at[i], upsem.at[i]) for i in range(9)]
    loc = [pltpu.make_async_copy(ulo_hbm.at[i], ulo.at[i], losem.at[i]) for i in range(16)]
    for i in (3, 4, 5, 6, 7, 8, 0, 1, 2):
        upc[i].start()
    for c in loc:
        c.start()
    body = pl.ds(PAD, cols)
    prev = pl.ds(PAD - 1, cols)
    nxt = pl.ds(PAD + 1, cols)
    zero8 = jnp.zeros((4, PAD, d), F32)
    hid[:, 0:PAD, :] = zero8
    hid[:, PAD + cols:, :] = zero8
    zact = jnp.zeros((6, 2, PAD, d), F32)
    act[:, :, 0:PAD, :] = zact
    act[:, :, PAD + cols:, :] = zact
    rest = proj_ref[256:]
    blank = jnp.zeros((64, d), BF)
    projx[0:64, 0:d] = rest
    projx[0:64, d : 2 * d] = blank
    projx[64:128, 0:d] = blank
    projx[64:128, d : 2 * d] = rest
    for i in range(4):
        extra = dot(canx_ref[i], projx[...])
        extra = jnp.concatenate(
            [extra[:, :d].reshape(cols // 16, 8, d), extra[:, d:].reshape(cols // 16, 8, d)], axis=1
        ).reshape(cols, d)
        v = (dot(can_ref[i], proj_ref[0:256]) + extra).astype(BF).astype(F32)
        hid[i, body, :] = v

    def three(load):
        mid = load(body)
        return [(load(prev) - mid).astype(BF), mid.astype(BF), (load(nxt) - mid).astype(BF)]

    def both(x, p):
        s = dot(x[1], uup[3 * p + 1])
        return s + dot(x[0], uup[3 * p]), s + dot(x[2], uup[3 * p + 2])

    def middle(k):
        e, o = both(three(lambda sl: hid[k, sl, :]), 1)
        ts[k % 2, 0] = e + bup_ref[...]
        ts[k % 2, 1] = o + bup_ref[...]

    def act_row(slot, par, v):
        half = 0.5 * v
        act[slot, par, body, :] = half + half * jnp.tanh(half)

    for i in (3, 4, 5):
        upc[i].wait()
    middle(0)
    for i in (6, 7, 8, 0, 1, 2):
        upc[i].wait()

    def step(k, _):
        x = three(lambda sl: hid[k + 1, sl, :] - hid[k, sl, :])
        down = both(x, 2)
        for par in range(2):
            act_row(2 * k, par, ts[k % 2, par] + down[par])
        middle(k + 1)
        up = both(x, 0)
        for par in range(2):
            act_row(2 * k + 1, par, ts[(k + 1) % 2, par] - up[par])
        return 0

    lax.fori_loop(0, 3, step, 0)

    @pl.when(first_dev)
    def _():
        act[0, :, body, :] = jnp.zeros((2, cols, d), F32)

    @pl.when(last_dev)
    def _():
        act[5, :, body, :] = jnp.zeros((2, cols, d), F32)

    for c in loc:
        c.wait()

    def products(r):
        one, two, sgn = ((0, 2, -1), (1, 2, 1), (2, 1, -1), (1, 3, -1))[r]
        vs = [[], [], [], []]
        for t in range(2):

            def ld(par, sl):
                u, v = act[2 * t + one, par, sl, :], act[2 * t + two, par, sl, :]
                return u + v if sgn > 0 else u - v

            ev = ld(0, body)
            od = ld(1, body)
            vs[0].append((ld(1, prev) - od).astype(BF))
            vs[1].append((ev + od).astype(BF))
            vs[2].append((od - ev).astype(BF))
            vs[3].append((ev - ld(0, nxt)).astype(BF))
        m = [dot(jnp.concatenate(vs[c], axis=0), ulo[4 * r + c]) for c in range(4)]
        plus, minus = m[1] + m[2], m[1] - m[2]
        y = [plus + m[0], minus - m[3]]
        return [[y[b][t * cols : (t + 1) * cols] for b in range(2)] for t in range(2)]

    ocp = [pltpu.make_async_copy(obuf.at[i], out_ref.at[i], osem.at[i]) for i in range(4)]

    def emit(t, a, b, v):
        for lane in range(0, d, 128):
            inter[2 * t + a, lane // 128, pl.ds(b, cols, stride=2), :] = v[:, lane : lane + 128]

    def flush(a):
        for t in range(2):
            for lane in range(0, d, 128):
                obuf[2 * t + a, :, lane : lane + 128] = inter[2 * t + a, lane // 128].astype(BF)
            ocp[2 * t + a].start()

    def inner_pair(_, carry):
        y = products(1)
        for t in range(2):
            h = hid[t + 1, body, :] + blo_ref[...]
            for b in range(2):
                v = h + y[t][b]
                acc[t, 0, b] = v
                acc[t, 1, b] = v
        y = products(2)
        for t in range(2):
            for b in range(2):
                acc[t, 0, b] += y[t][b]
                acc[t, 1, b] -= y[t][b]
        return carry

    def outer_pair(_, carry):
        y = products(0)
        for t in range(2):
            for b in range(2):
                emit(t, 0, b, acc[t, 0, b] + y[t][b])
        flush(0)
        y = products(3)
        for t in range(2):
            for b in range(2):
                emit(t, 1, b, acc[t, 1, b] - y[t][b])
        flush(1)
        return carry

    once = 1 + row // lax.axis_size("row")
    lax.fori_loop(0, once, inner_pair, 0)
    outer_pair(0, 0)
    for c in ocp:
        c.wait()


def decode(canvas, extra, proj, uup, bup, ulo, blo):
    cols, d = canvas.shape[1], proj.shape[1]
    return pl.pallas_call(
        functools.partial(decode_kernel, cols, d),
        out_shape=jax.ShapeDtypeStruct((4, 2 * cols, d), BF),
        in_specs=[VM, VM, VM, HB, VM, HB, VM],
        out_specs=HB,
        scratch_shapes=[
            pltpu.VMEM((4, cols + 2 * PAD, d), F32),
            pltpu.VMEM((6, 2, cols + 2 * PAD, d), F32),
            pltpu.VMEM((2, 2, cols, d), F32),
            pltpu.VMEM((2, 2, 2, cols, d), F32),
            pltpu.VMEM((4, d // 128, 2 * cols, 128), F32),
            pltpu.VMEM((128, 2 * d), BF),
            pltpu.VMEM((4, 2 * cols, d), BF),
            pltpu.VMEM((9, d, d), BF),
            pltpu.VMEM((16, d, d), BF),
            pltpu.SemaphoreType.DMA((9,)),
            pltpu.SemaphoreType.DMA((16,)),
            pltpu.SemaphoreType.DMA((4,)),
        ],
        compiler_params=pltpu.CompilerParams(vmem_limit_bytes=60 * 2**20),
        name="decode",
    )(canvas, extra, proj, uup, bup, ulo, blo)


def on_device(
    latent,
    tile_reach,
    first_weight,
    first_bias,
    second_weight,
    second_bias,
    proj_weight,
    upper_weight,
    upper_bias,
    lower_weight,
    lower_bias,
):
    canvas, extra, uup, ulo = front(
        tile_reach.transpose(0, 2, 1),
        latent,
        first_weight,
        first_bias,
        second_weight,
        second_bias,
        upper_weight,
        lower_weight,
    )
    return decode(canvas, extra, proj_weight, uup, upper_bias[None], ulo, lower_bias[None])


def solution(mesh):
    in_specs = (P("row", "col"), P(), P(), P(), P(), P(), P(), P(), P(), P(), P())
    out_specs = P(("row", "col"), None, None)
    return jax.shard_map(on_device, mesh=mesh, in_specs=in_specs, out_specs=out_specs, check_vma=False)
```

profile of v0, /device:TPU:1, one launch (start us, length us, event | category | flops | bytes accessed | tf_op | source)
XLA Modules:
  0.0 60.0 jit_solution(15891790646383555486)
XLA Ops:
  0.0 41.7 %front.1 = (bf16[4,256,256]{2,1,0:T(8,128)(2,1)}, bf16[4,128,128]{2,1,0:T(8,128)(2,1)}, bf16[9,512,512]{2,1,0:T(8,128)(2,1)}, bf16[16,512,512]{2,1,0:T(8,128)(2,1)}) custom-call(s32[8,4,16]{2,1,0:T(4,128)} %bitcast.7, bf16[32,5120]{1,0:T(8,128)(2,1)} %lat_ref.1, bf16[3,960,320]{2,1,0:T(8,128)(2,1)} %bitcast.5, f32[320]{0:T(512)} %b1_ref.1, ...), custom_call_target="tpu_custom_call" | custom-call | tf_op jit(solution)/shard_map/front/pallas_call | solution.py:396
  41.7 18.1 %decode.1 = bf16[4,512,512]{2,1,0:T(8,128)(2,1)} custom-call(bf16[4,256,256]{2,1,0:T(8,128)(2,1)} %get-tuple-element.9.can_ref, bf16[4,128,128]{2,1,0:T(8,128)(2,1)} %get-tuple-element.10.canx_ref, bf16[320,512]{1,0:T(8,128)(2,1)} %proj_ref.1, bf16[9,512,512]{2,1,0:T(8,128)(2,1)} %get-tuple-element.11.uup_hbm, f32[1,512]{1,0:T(1,128)} %bitcast.8, ...), custom_call_target="tpu_custom_call" | custom-call | tf_op jit(solution)/shard_map/decode/pallas_call | solution.py:598
where the time goes:
time: 60.1 us; the launch traced here: 60 us
  Pallas kernels  59.8 us (100%)
    pallas_call x1, Pallas kernels, front(): pl.pallas_call(front_kernel, out_shape=[jax.ShapeDtypeStruct((deep, n_col...  41.7 us
    pallas_call x1, Pallas kernels, decode(): pl.pallas_call(functools.partial(decode_kernel, cols, d), out_shape=jax.S...  18.1 us

commit v1 on v0

--- a/solution.py
+++ b/solution.py
@@ -356,11 +356,12 @@
             )
         ]
 
-    copies = []
-    for o in range(1, n_col):
+    copies = {}
+    order = sorted(range(1, n_col), key=lambda o: abs(2 * o - n_col))
+    for o in order:
         to = peer(row, col, 0, o)
-        copies.append(send_rows(to, step * to[1], mine, minex, o))
-        for c in copies[-1]:
+        copies[o] = send_rows(to, step * to[1], mine, minex, o)
+        for c in copies[o]:
             c.start()
     loads[3].wait()
     forms(lower_forms, lo, vo, vo_hbm, vsem)
@@ -372,7 +373,7 @@
         src = peer(row, col, 0, -o)
         spot = pl.ds(pl.multiple_of(cols * src[1], cols), cols)
         spotx = pl.ds(pl.multiple_of(8 * src[1], 8), 8)
-        for c in copies[o - 1]:
+        for c in copies[o]:
             c.wait_send()
         for c in send_rows(src, 0, spot, spotx, o):
             c.wait_recv()
@@ -402,7 +403,7 @@
             jax.ShapeDtypeStruct((16, d, d), BF),
         ],
         in_specs=[SM, VM, HB, VM, HB, VM, HB, HB],
-        out_specs=[VM, VM, HB, HB],
+        out_specs=[HB, HB, HB, HB],
         scratch_shapes=around(rows, m)
         + around(tall, m + 1)
         + [
@@ -445,13 +446,23 @@
     )(reach, latent, w1, b1, w2, b2, upper, lower)
 
 
-def decode_kernel(cols, d, can_ref, canx_ref, proj_ref, uup_hbm, bup_ref, ulo_hbm, blo_ref, out_ref,
-                  hid, act, ts, acc, inter, projx, obuf, uup, ulo, upsem, losem, osem):
+def decode_kernel(cols, d, can_hbm, canx_hbm, proj_ref, uup_hbm, bup_ref, ulo_hbm, blo_ref, out_ref,
+                  hid, act, ts, acc, inter, projx, obuf, can_ref, canx_ref, uup, ulo, upsem, losem, osem, csem, xsem):
     row, col = lax.axis_index("row"), lax.axis_index("col")
     first_dev = (row == 0) & (col == 0)
     last_dev = (row == lax.axis_size("row") - 1) & (col == lax.axis_size("col") - 1)
     upc = [pltpu.make_async_copy(uup_hbm.at[i], uup.at[i], upsem.at[i]) for i in range(9)]
     loc = [pltpu.make_async_copy(ulo_hbm.at[i], ulo.at[i], losem.at[i]) for i in range(16)]
+    rows_in = [
+        (
+            pltpu.make_async_copy(can_hbm.at[i], can_ref.at[i], csem.at[i]),
+            pltpu.make_async_copy(canx_hbm.at[i], canx_ref.at[i], xsem.at[i]),
+        )
+        for i in range(4)
+    ]
+    for pair in rows_in:
+        for c in pair:
+            c.start()
     for i in (3, 4, 5, 6, 7, 8, 0, 1, 2):
         upc[i].start()
     for c in loc:
@@ -472,6 +483,8 @@
     projx[64:128, 0:d] = blank
     projx[64:128, d : 2 * d] = rest
     for i in range(4):
+        for c in rows_in[i]:
+            c.wait()
         extra = dot(canx_ref[i], projx[...])
         extra = jnp.concatenate(
             [extra[:, :d].reshape(cols // 16, 8, d), extra[:, d:].reshape(cols // 16, 8, d)], axis=1
@@ -598,7 +611,7 @@
     return pl.pallas_call(
         functools.partial(decode_kernel, cols, d),
         out_shape=jax.ShapeDtypeStruct((4, 2 * cols, d), BF),
-        in_specs=[VM, VM, VM, HB, VM, HB, VM],
+        in_specs=[HB, HB, VM, HB, VM, HB, VM],
         out_specs=HB,
         scratch_shapes=[
             pltpu.VMEM((4, cols + 2 * PAD, d), F32),
@@ -608,10 +621,14 @@
             pltpu.VMEM((4, d // 128, 2 * cols, 128), F32),
             pltpu.VMEM((128, 2 * d), BF),
             pltpu.VMEM((4, 2 * cols, d), BF),
+            pltpu.VMEM(canvas.shape, BF),
+            pltpu.VMEM(extra.shape, BF),
             pltpu.VMEM((9, d, d), BF),
             pltpu.VMEM((16, d, d), BF),
             pltpu.SemaphoreType.DMA((9,)),
             pltpu.SemaphoreType.DMA((16,)),
+            pltpu.SemaphoreType.DMA((4,)),
+            pltpu.SemaphoreType.DMA((4,)),
             pltpu.SemaphoreType.DMA((4,)),
         ],
         compiler_params=pltpu.CompilerParams(vmem_limit_bytes=60 * 2**20),

time: 60.1 us -> 60.9 us (1.013)
  Pallas kernels: 59.8 us -> 60.6 us
    pallas_call x1, Pallas kernels: 18.1 us -> 18.9 us  [decode(): pl.pallas_call(functools.partial(decode_kernel, cols, d), out_shape=jax.S...]
where the time goes in v1:
time: 60.9 us; the launch traced here: 60.8 us
  Pallas kernels  60.6 us (100%)
    pallas_call x1, Pallas kernels, front(): pl.pallas_call(front_kernel, out_shape=[jax.ShapeDtypeStruct((deep, n_col...  41.8 us
    pallas_call x1, Pallas kernels, decode(): pl.pallas_call(functools.partial(decode_kernel, cols, d), out_shape=jax.S...  18.9 us

profile of v1, /device:TPU:1, one launch (start us, length us, event | category | flops | bytes accessed | tf_op | source)
XLA Modules:
  0.0 60.8 jit_solution(795524498476595516)
XLA Ops:
  0.0 41.8 %front.1 = (bf16[4,256,256]{2,1,0:T(8,128)(2,1)}, bf16[4,128,128]{2,1,0:T(8,128)(2,1)}, bf16[9,512,512]{2,1,0:T(8,128)(2,1)}, bf16[16,512,512]{2,1,0:T(8,128)(2,1)}) custom-call(s32[8,4,16]{2,1,0:T(4,128)} %bitcast.7, bf16[32,5120]{1,0:T(8,128)(2,1)} %lat_ref.1, bf16[3,960,320]{2,1,0:T(8,128)(2,1)} %bitcast.5, f32[320]{0:T(512)} %b1_ref.1, ...), custom_call_target="tpu_custom_call" | custom-call | tf_op jit(solution)/shard_map/front/pallas_call | solution.py:397
  41.8 18.9 %decode.1 = bf16[4,512,512]{2,1,0:T(8,128)(2,1)} custom-call(bf16[4,256,256]{2,1,0:T(8,128)(2,1)} %get-tuple-element.9.can_hbm, bf16[4,128,128]{2,1,0:T(8,128)(2,1)} %get-tuple-element.10.canx_hbm, bf16[320,512]{1,0:T(8,128)(2,1)} %proj_ref.1, bf16[9,512,512]{2,1,0:T(8,128)(2,1)} %get-tuple-element.11.uup_hbm, f32[1,512]{1,0:T(1,128)} %bitcast.8, ...), custom_call_target="tpu_custom_call" | custom-call | tf_op jit(solution)/shard_map/decode/pallas_call | solution.py:611

commit v2 on v0

--- a/solution.py
+++ b/solution.py
@@ -356,11 +356,12 @@
             )
         ]
 
-    copies = []
-    for o in range(1, n_col):
+    copies = {}
+    order = sorted(range(1, n_col), key=lambda o: abs(2 * o - n_col))
+    for o in order:
         to = peer(row, col, 0, o)
-        copies.append(send_rows(to, step * to[1], mine, minex, o))
-        for c in copies[-1]:
+        copies[o] = send_rows(to, step * to[1], mine, minex, o)
+        for c in copies[o]:
             c.start()
     loads[3].wait()
     forms(lower_forms, lo, vo, vo_hbm, vsem)
@@ -372,7 +373,7 @@
         src = peer(row, col, 0, -o)
         spot = pl.ds(pl.multiple_of(cols * src[1], cols), cols)
         spotx = pl.ds(pl.multiple_of(8 * src[1], 8), 8)
-        for c in copies[o - 1]:
+        for c in copies[o]:
             c.wait_send()
         for c in send_rows(src, 0, spot, spotx, o):
             c.wait_recv()
@@ -402,7 +403,7 @@
             jax.ShapeDtypeStruct((16, d, d), BF),
         ],
         in_specs=[SM, VM, HB, VM, HB, VM, HB, HB],
-        out_specs=[VM, VM, HB, HB],
+        out_specs=[HB, HB, HB, HB],
         scratch_shapes=around(rows, m)
         + around(tall, m + 1)
         + [

time: 60.1 us -> 60.2 us (level)
  no operation moved by 1% of the time
where the time goes in v2:
time: 60.2 us; the launch traced here: 60.1 us
  Pallas kernels  59.9 us (100%)
    pallas_call x1, Pallas kernels, front(): pl.pallas_call(front_kernel, out_shape=[jax.ShapeDtypeStruct((deep, n_col...  41.8 us
    pallas_call x1, Pallas kernels, decode(): pl.pallas_call(functools.partial(decode_kernel, cols, d), out_shape=jax.S...  18.1 us

profile of v2, /device:TPU:1, one launch (start us, length us, event | category | flops | bytes accessed | tf_op | source)
XLA Modules:
  0.0 60.1 jit_solution(7680038759317374379)
XLA Ops:
  0.0 41.8 %front.1 = (bf16[4,256,256]{2,1,0:T(8,128)(2,1)}, bf16[4,128,128]{2,1,0:T(8,128)(2,1)}, bf16[9,512,512]{2,1,0:T(8,128)(2,1)}, bf16[16,512,512]{2,1,0:T(8,128)(2,1)}) custom-call(s32[8,4,16]{2,1,0:T(4,128)} %bitcast.7, bf16[32,5120]{1,0:T(8,128)(2,1)} %lat_ref.1, bf16[3,960,320]{2,1,0:T(8,128)(2,1)} %bitcast.5, f32[320]{0:T(512)} %b1_ref.1, ...), custom_call_target="tpu_custom_call" | custom-call | tf_op jit(solution)/shard_map/front/pallas_call | solution.py:397
  41.8 18.1 %decode.1 = bf16[4,512,512]{2,1,0:T(8,128)(2,1)} custom-call(bf16[4,256,256]{2,1,0:T(8,128)(2,1)} %get-tuple-element.9.can_ref, bf16[4,128,128]{2,1,0:T(8,128)(2,1)} %get-tuple-element.10.canx_ref, bf16[320,512]{1,0:T(8,128)(2,1)} %proj_ref.1, bf16[9,512,512]{2,1,0:T(8,128)(2,1)} %get-tuple-element.11.uup_hbm, f32[1,512]{1,0:T(1,128)} %bitcast.8, ...), custom_call_target="tpu_custom_call" | custom-call | tf_op jit(solution)/shard_map/decode/pallas_call | solution.py:599
